TPU v7x, 128 devices: a whole 4x4x4 slice. The times are simulated.
128 devices in a mesh: region: 16 (over y, z_hi, core), pos: 8 (over z_lo, x).
Axes of the slice: x: 4, y: 4, z: 4 (z_hi: 2, z_lo: 2; z = z_hi * 2 + z_lo), core: 2. Of those that a mesh axis runs over, the one named last changes fastest.
Arguments:
- object_tiles: float32 [256, 2, 2, 128, 128], P('region'), may hold values from -4 to 4
- probe: float32 [4, 2, 256, 256], replicated, may hold values from -3 to 3
- fresnel_phase: float32 [256, 256], replicated, may hold values from -3.140625 to 3.140625
- patterns: float32 [16, 8, 2, 256, 256], P('region', 'pos'), may hold values from 0 to 4
- row_offsets: int32 [16, 8, 2], P('region', 'pos'), may hold values from 0 to 3840, as said below
- col_offsets: int32 [16, 8, 2], P('region', 'pos'), may hold values from 0 to 768
- counts: int32 [16, 8], P('region', 'pos'), may hold values from 1 to 2, as said below
Outputs:
- new_object: float32 [256, 2, 2, 128, 128], P('region')
Inputs may be any that keep to these rules, and one draw needn't show every extreme that they name: A device's live positions are its first counts slots; the other slots of its position arrays are ignored. Some device holds 2 live positions. `row_offsets`: every slot of region index r starts at a row from r * 2 * 128 to r * 2 * 128 + 2 * 128 - 1, and never after row 3840.
All inputs are finite; a program needn't handle non-finite values.
Results may differ from a plain program's by a relative error of at most 0.0095.
Values sent between devices are 32-bit elements; how exact they have to be, the bound alone decides.
No kernel may reach another device: no remote copies, remote signals or barrier semaphores. Data moves between devices by JAX's collectives and lax.ppermute only.
A program may use at most 128 MiB of HBM per device.

v0:
```python
import math
import jax
import jax.numpy as jnp
from jax import lax
from jax.sharding import PartitionSpec as P

TGX = 8
step_size = 0.05


def shifted(shard, axis, by):
    count = lax.axis_size(axis)
    pairs = [(i, i + by) for i in range(count) if 0 <= i + by < count]
    return lax.ppermute(shard, axis, pairs)


def make_tables(length):
    counter = jnp.arange(length, dtype=jnp.int32)
    product = counter[:, None] * counter[None, :] % length
    angles = product.astype(jnp.float32) * jnp.float32(2.0 * math.pi / length)
    factor = jnp.float32(1.0 / math.sqrt(length))
    return (
        (jnp.cos(angles) * factor).astype(jnp.bfloat16),
        (jnp.sin(angles) * factor).astype(jnp.bfloat16),
    )


def left_product(matrix, field):
    return jnp.einsum("jk,mkl->mjl", matrix, field, preferred_element_type=jnp.float32)


def right_product(field, matrix):
    return jnp.einsum("mjk,kl->mjl", field, matrix, preferred_element_type=jnp.float32)


def transform(field_re, field_im, direction, cos_table, sin_table):
    upper_re = left_product(cos_table, field_re) - direction * left_product(sin_table, field_im)
    upper_im = left_product(cos_table, field_im) + direction * left_product(sin_table, field_re)
    upper_re = upper_re.astype(jnp.bfloat16)
    upper_im = upper_im.astype(jnp.bfloat16)
    result_re = right_product(upper_re, cos_table) - direction * right_product(upper_im, sin_table)
    result_im = right_product(upper_im, cos_table) + direction * right_product(upper_re, sin_table)
    return (result_re, result_im)


def complex_product(left_re, left_im, right_re, right_im):
    return (left_re * right_re - left_im * right_im, left_re * right_im + left_im * right_re)


def conj_product(left_re, left_im, right_re, right_im):
    return (left_re * right_re + left_im * right_im, left_re * right_im - left_im * right_re)


def position_gradient(patch, probe, wave_re, wave_im, measured, cos_table, sin_table):
    slice_count = patch.shape[0]
    field_re = probe[:, 0]
    field_im = probe[:, 1]
    incoming = []
    for layer_index in range(slice_count):
        incoming.append((field_re, field_im))
        exit_re, exit_im = complex_product(
            field_re, field_im, patch[layer_index, 0], patch[layer_index, 1]
        )
        exit_re = exit_re.astype(jnp.bfloat16)
        exit_im = exit_im.astype(jnp.bfloat16)
        if layer_index + 1 < slice_count:
            spec_re, spec_im = transform(exit_re, exit_im, -1.0, cos_table, sin_table)
            spec_re, spec_im = complex_product(wave_re, wave_im, spec_re, spec_im)
            field_re, field_im = transform(
                spec_re.astype(jnp.bfloat16),
                spec_im.astype(jnp.bfloat16),
                1.0,
                cos_table,
                sin_table,
            )
    far_re, far_im = transform(exit_re, exit_im, -1.0, cos_table, sin_table)
    intensity = jnp.sum(far_re * far_re + far_im * far_im, axis=0)
    misfit = intensity - measured
    back_re, back_im = transform(
        (misfit * far_re).astype(jnp.bfloat16),
        (misfit * far_im).astype(jnp.bfloat16),
        1.0,
        cos_table,
        sin_table,
    )
    results = [None] * slice_count
    for layer_index in reversed(range(slice_count)):
        incident_re, incident_im = incoming[layer_index]
        grad_re, grad_im = conj_product(incident_re, incident_im, back_re, back_im)
        results[layer_index] = jnp.stack([jnp.sum(grad_re, axis=0), jnp.sum(grad_im, axis=0)])
        if layer_index > 0:
            prior_re, prior_im = conj_product(
                patch[layer_index, 0], patch[layer_index, 1], back_re, back_im
            )
            spec_re, spec_im = transform(
                prior_re.astype(jnp.bfloat16),
                prior_im.astype(jnp.bfloat16),
                -1.0,
                cos_table,
                sin_table,
            )
            spec_re, spec_im = conj_product(wave_re, wave_im, spec_re, spec_im)
            back_re, back_im = transform(
                spec_re.astype(jnp.bfloat16),
                spec_im.astype(jnp.bfloat16),
                1.0,
                cos_table,
                sin_table,
            )
    return jnp.stack(results)


def tiles_to_band(tiles, band_tiles, tile_side):
    slice_count = tiles.shape[1]
    across = tiles.shape[0] // band_tiles
    shaped = tiles.reshape(band_tiles, across, slice_count, 2, tile_side, tile_side).transpose(
        2, 3, 0, 4, 1, 5
    )
    return shaped.reshape(slice_count, 2, band_tiles * tile_side, across * tile_side)


def per_device(object_tiles, probe, fresnel_phase, patterns, row_offsets, col_offsets, counts):
    slot_count = patterns.shape[2]
    pattern_side = patterns.shape[-1]
    tile_side = object_tiles.shape[-1]
    slice_count = object_tiles.shape[1]
    held_tiles = object_tiles.shape[0]
    band_tiles = held_tiles // TGX
    band_rows = band_tiles * tile_side
    width_pixels = TGX * tile_side
    measured = patterns.reshape(slot_count, pattern_side, pattern_side)
    row_start = row_offsets.reshape(slot_count)
    col_start = col_offsets.reshape(slot_count)
    live_count = counts.reshape(())
    following = shifted(object_tiles, "region", -1)
    canvas = jnp.concatenate(
        [
            tiles_to_band(object_tiles, band_tiles, tile_side),
            tiles_to_band(following, band_tiles, tile_side),
        ],
        axis=2,
    )
    band_first = lax.axis_index("region") * band_rows
    cos_table, sin_table = make_tables(pattern_side)
    wave_re = jnp.cos(fresnel_phase)
    wave_im = jnp.sin(fresnel_phase)
    zero_index = jnp.int32(0)

    def one_position(position, gradient):
        local_row = row_start[position] - band_first
        local_col = col_start[position]
        corner = (zero_index, zero_index, local_row, local_col)
        patch = lax.dynamic_slice(canvas, corner, (slice_count, 2, pattern_side, pattern_side))
        term = position_gradient(
            patch, probe, wave_re, wave_im, measured[position], cos_table, sin_table
        )
        former = lax.dynamic_slice(gradient, corner, (slice_count, 2, pattern_side, pattern_side))
        return lax.dynamic_update_slice(gradient, former + term, corner)

    empty = jnp.zeros((slice_count, 2, 2 * band_rows, width_pixels), jnp.float32)
    gradient = lax.fori_loop(0, live_count, one_position, empty)
    shaped = gradient.reshape(slice_count, 2, 2, band_tiles, tile_side, TGX, tile_side).transpose(
        2, 3, 5, 0, 1, 4, 6
    )
    shaped = shaped.reshape(2, held_tiles * slice_count * 2 * tile_side, tile_side)
    own_rows = shaped[0]
    spill_rows = shaped[1]
    held_rows = object_tiles.reshape(-1, tile_side)
    arrived = shifted(spill_rows, "region", 1)
    combined = lax.psum(own_rows + arrived, "pos")
    return (held_rows - step_size * combined).reshape(object_tiles.shape)


def solution(mesh):
    in_specs = (
        P("region", None, None, None, None),
        P(),
        P(),
        P("region", "pos", None, None, None),
        P("region", "pos", None),
        P("region", "pos", None),
        P("region", "pos"),
    )
    out_specs = P("region", None, None, None, None)
    return jax.shard_map(
        per_device, mesh=mesh, in_specs=in_specs, out_specs=out_specs, check_vma=False
    )
```

profile of v0, /device:TPU:1, one launch (start us, length us, event | category | flops | bytes accessed | tf_op | source)
XLA Modules:
  0.0 442.0 jit_solution(3993360952174075984)
XLA Ops:
  6.5 3.3 collective-permute-start
  9.8 1.9 copy.58
  12.7 4.4 copy.113
  17.0 4.9 %reshape.50 = f32[2,2,256,1024]{3,2,1,0:T(8,128)} reshape(f32[2,2,2,128,8,128]{5,4,3,2,1,0:T(8,128)} %bitcast.461) | data formatting | bytes 8388608 | tf_op jit(solution)/shard_map/reshape | solution.py:119
  22.0 1.6 fusion.370
  23.6 36.4 %collective-permute-done = f32[16,2,2,128,128]{4,3,2,1,0:T(8,128)} collective-permute-done((f32[16,2,2,128,128]{4,3,2,1,0:T(8,128)}, f32[16,2,2,128,128]{4,3,2,1,0:T(8,128)}, u32[]{:S(2)}, u32[]{:S(2)}) %collective-permute-start) | collective-permute-done | bytes 4194336 | tf_op jit(solution)/shard_map/ppermute | solution.py:14
  59.9 6.6 %copy.112 = f32[2,8,2,2,128,128]{5,1,4,0,3,2:T(8,128)} copy(f32[2,8,2,2,128,128]{5,4,3,2,1,0:T(8,128)} %bitcast.6) | data formatting | bytes 8388608 | tf_op jit(solution)/shard_map/reshape | solution.py:116
  66.5 4.9 %reshape.52 = f32[2,2,256,1024]{3,2,1,0:T(8,128)} reshape(f32[2,2,2,128,8,128]{5,4,3,2,1,0:T(8,128)} %bitcast.460) | data formatting | bytes 8388608 | tf_op jit(solution)/shard_map/reshape | solution.py:119
  71.4 8.3 %pad_maximum_fusion = f32[2,2,512,1024]{3,2,1,0:T(8,128)} fusion(f32[2,2,256,1024]{3,2,1,0:T(8,128)} %reshape.52, f32[2,2,256,1024]{3,2,1,0:T(8,128)} %reshape.50), kind=kLoop, calls=%fused_computation.377 | loop fusion | flops 2097152 | bytes 16777216 | tf_op jit(solution)/shard_map/concatenate | solution.py:136
  79.7 4.3 broadcast_in_dim.2
  84.0 93.7 %while.12 = (s32[]{:T(128)}, f32[2,2,512,1024]{3,2,1,0:T(8,128)}, s32[]{:T(128)}, s32[2]{0:T(128)S(1)}, s32[]{:T(128)}, /*index=5*/s32[2]{0:T(128)S(1)}, f32[4,2...) while((s32[]{:T(128)}, f32[2,2,512,1024]{3,2,1,0:T(8,128)}, ...), condition=%wide.region_6.7_spmd.clone.clone, body=%wide.region_0.6_spmd.clone.clone.sunk | while | flops 6523715584 | bytes 125305184 | solution.py:161
  89.0 1.7 dynamic-slice_bitcast_fusion.5
  99.8 2.5 subtract_convert_fusion.7
  103.5 1.4 fusion.638
  111.2 1.5 subtract_convert_fusion.8
  115.2 1.5 fusion.646
  121.7 1.3 add_reduce_fusion.3
  125.3 1.3 fusion.655
  127.9 1.3 fusion.652
  129.2 1.7 fusion.653
  133.4 1.9 subtract_convert_fusion.9
  142.8 1.4 fusion.662
  144.3 2.4 add_convert_fusion.5
  155.5 1.6 fusion.670
  157.2 1.8 maximum_add_fusion.2
  159.0 12.2 %dynamic_update_slice.6 = f32[2,2,512,1024]{3,2,1,0:T(8,128)} dynamic-update-slice(f32[2,2,512,1024]{3,2,1,0:T(8,128)} %get-tuple-element.510, f32[2,2,256,256]{3,2,1,0:T(8,128)S(1)} %maximum_add_fusion.2, s32[]{:T(128)} %constant.14.clone.1..sunk, s32[]{:T(128)} %constant.14.clone.1..sunk, s32[]{:T(128)S(6)} %select_n.300, s32[]{:T(128)S(6)} %select_n.301) | dynamic-update-slice | bytes 2097156 | tf_op jit(solution)/shard_map/while/body/dynamic_update_slice | solution.py:158
  177.8 5.5 %copy.109 = f32[256,8,8,128]{3,2,1,0:T(8,128)S(1)} copy(f32[256,8,8,128]{3,1,2,0:T(8,128)} %bitcast.455) | data formatting | bytes 16777216
  184.8 1.9 collective-permute-start.1
  187.6 44.6 %collective-permute-done.1 = f32[8192,128]{1,0:T(8,128)S(1)} collective-permute-done((f32[8192,128]{1,0:T(8,128)S(1)}, f32[8192,128]{1,0:T(8,128)S(1)}, u32[]{:S(2)}, u32[]{:S(2)}) %collective-permute-start.1) | collective-permute-done | bytes 4194336 | tf_op jit(solution)/shard_map/ppermute | solution.py:14
  232.2 2.4 bitcast_add_fusion
  234.6 194.3 %all-reduce.2.cloned.1.call-done = f32[8192,128]{1,0:T(8,128)} async-done(((f32[8192,128]{1,0:T(8,128)}), f32[8192,128]{1,0:T(8,128)}) %all-reduce.2.cloned.1.call-update) | async-done | bytes 4194320 | tf_op jit(solution)/shard_map/psum | solution.py:170
  428.9 6.0 %bitcast_subtract_fusion.1 = f32[8192,128]{1,0:T(8,128)} fusion(f32[16,2,2,128,128]{4,3,2,1,0:T(8,128)} %param.9, f32[8192,128]{1,0:T(8,128)} %all-reduce.2.cloned.1.call-done), kind=kLoop, calls=%fused_computation.379 | loop fusion | flops 2097152 | bytes 12582912 | tf_op jit(solution)/shard_map/sub | solution.py:171
  (54 shorter events, 51.0 us)
Async XLA Ops:
  6.5 422.4 %all-reduce.2.cloned.1.call-start = ((), (), s32[]{:S(2)}) async-start(), calls=%async_computation | async-start | bytes 8388608 | tf_op jit(solution)/shard_map/psum | solution.py:170
  6.5 53.4 %collective-permute-start = (f32[16,2,2,128,128]{4,3,2,1,0:T(8,128)}, f32[16,2,2,128,128]{4,3,2,1,0:T(8,128)}, u32[]{:S(2)}, u32[]{:S(2)}) collective-permute-start(f32[16,2,2,128,128]{4,3,2,1,0:T(8,128)} %param.9), channel_id=1, source_target_pairs={{8,0},{16,8},{24,16},{32,24},{40,32},{48,40},{56,48},{64,56},{72,6... | collective-permute-start | bytes 12582920 | tf_op jit(solution)/shard_map/ppermute | solution.py:14
  9.8 2.8 copy-start
  17.0 4.9 %copy-start.1 = (f32[256,256]{1,0:T(8,128)S(1)}, f32[256,256]{1,0:T(8,128)}, u32[]{:S(2)}) copy-start(f32[256,256]{1,0:T(8,128)} %param.11) | copy-start | bytes 786436
  79.7 4.3 copy-start.2
  79.7 4.3 copy-start.3
  184.8 47.4 %collective-permute-start.1 = (f32[8192,128]{1,0:T(8,128)S(1)}, f32[8192,128]{1,0:T(8,128)S(1)}, u32[]{:S(2)}, u32[]{:S(2)}) collective-permute-start(f32[8192,128]{1,0:T(8,128)S(1)} %bitcast.464), channel_id=1, source_target_pairs={{0,8},{8,16},{16,24},{24,32},{32,40},{40,48},{48,56},{56,64},{64,7... | collective-permute-start | bytes 12582920 | tf_op jit(solution)/shard_map/ppermute | solution.py:14
Sparse Core Ops, SparseCore 0:
  234.7 194.1 all-reduce.1
where the time goes:
time: 449 us; the launch traced here: 442 us
  waiting for transfers between devices  275 us (61%)
  matrix products  64.9 us (14%)
  local copies, waits for them, and re-layouts  52.4 us (12%)
  other arithmetic  19.9 us (4%)
  between operations  13.7 us (3%)
  loops' own time  10.6 us (2%)
  starting transfers between devices  5.2 us (1%)
    psum x1, waiting for transfers between devices, per_device(): combined = lax.psum(own_rows + arrived, 'pos')  194 us
    ppermute x2, waiting for transfers between devices, shifted(): return lax.ppermute(shard, axis, pairs)  81 us
    dot_general x24, matrix products, right_product(): jnp.einsum('mjk,kl->mjl', field, matrix, preferred_element_type=jnp.float32)  34.4 us
    dot_general x24, matrix products, left_product(): jnp.einsum('jk,mkl->mjl', matrix, field, preferred_element_type=jnp.float32)  30.5 us
    dynamic_update_slice x1, local copies, waits for them, and re-layouts, one_position(): return lax.dynamic_update_slice(gradient, former + term, corner)  12.2 us
    reshape x2, local copies, waits for them, and re-layouts, tiles_to_band(): tiles.reshape(band_tiles, across, slice_count, 2, tile_side, tile_side)  11 us
    another operation x1, loops' own time, per_device(): gradient = lax.fori_loop(0, live_count, one_position, empty)  10.6 us
    reshape x2, local copies, waits for them, and re-layouts, tiles_to_band(): shaped.reshape(slice_count, 2, band_tiles * tile_side, across * tile_side)  9.81 us
  transfers between devices with their start and end apart: 3, of which 3 were waited for; matrix products, arithmetic and copies ran while one was open for 3% of the time, Pallas kernels for 0%

commit v1 on v0

--- a/solution.py
+++ b/solution.py
@@ -167,7 +167,7 @@
     spill_rows = shaped[1]
     held_rows = object_tiles.reshape(-1, tile_side)
     arrived = shifted(spill_rows, "region", 1)
-    combined = lax.psum(own_rows + arrived, "pos")
+    combined = jnp.sum(lax.all_gather(own_rows + arrived, "pos"), axis=0)
     return (held_rows - step_size * combined).reshape(object_tiles.shape)
 
 

time: 449 us -> 687 us (1.53)
  waiting for transfers between devices: 275 us -> 498 us
  other arithmetic: 19.9 us -> 33.4 us
    all_gather x0 -> x1, waiting for transfers between devices: none -> 417 us  [per_device(): combined = jnp.sum(lax.all_gather(own_rows + arrived, 'pos'), axis=0)]
    psum x1 -> x0, waiting for transfers between devices: 194 us -> none  [per_device(): combined = lax.psum(own_rows + arrived, 'pos')]
    reduce_sum x0 -> x1, other arithmetic: none -> 14 us  [per_device(): combined = jnp.sum(lax.all_gather(own_rows + arrived, 'pos'), axis=0)]
  transfers between devices with their start and end apart: 3 -> 3, of which waited for: 3 -> 3; matrix products, arithmetic and copies ran while one was open for 3% -> 2% of each run, Pallas kernels for 0% -> 0%
where the time goes in v1:
time: 687 us; the launch traced here: 679 us
  waiting for transfers between devices  498 us (72%)
  matrix products  64.9 us (9%)
  local copies, waits for them, and re-layouts  53.2 us (8%)
  other arithmetic  33.4 us (5%)
  between operations  13.7 us (2%)
  loops' own time  11.3 us (2%)
    all_gather x1, waiting for transfers between devices, per_device(): combined = jnp.sum(lax.all_gather(own_rows + arrived, 'pos'), axis=0)  417 us
    ppermute x2, waiting for transfers between devices, shifted(): return lax.ppermute(shard, axis, pairs)  80.9 us
    dot_general x24, matrix products, right_product(): jnp.einsum('mjk,kl->mjl', field, matrix, preferred_element_type=jnp.float32)  34.4 us
    dot_general x24, matrix products, left_product(): jnp.einsum('jk,mkl->mjl', matrix, field, preferred_element_type=jnp.float32)  30.5 us
    reduce_sum x1, other arithmetic, per_device(): combined = jnp.sum(lax.all_gather(own_rows + arrived, 'pos'), axis=0)  14 us
  transfers between devices with their start and end apart: 3, of which 3 were waited for; matrix products, arithmetic and copies ran while one was open for 2% of the time, Pallas kernels for 0%

profile of v1, /device:TPU:1, one launch (start us, length us, event | category | flops | bytes accessed | tf_op | source)
XLA Modules:
  0.0 679.5 jit_solution(8731446998546547487)
XLA Ops:
  6.5 3.3 collective-permute-start
  9.8 1.9 copy.160
  12.7 4.4 copy.215
  17.0 4.9 reshape.48
  22.0 1.6 fusion.370
  23.6 36.3 %collective-permute-done = f32[16,2,2,128,128]{4,3,2,1,0:T(8,128)} collective-permute-done((f32[16,2,2,128,128]{4,3,2,1,0:T(8,128)}, f32[16,2,2,128,128]{4,3,2,1,0:T(8,128)}, u32[]{:S(2)}, u32[]{:S(2)}) %collective-permute-start) | collective-permute-done | bytes 4194336 | tf_op jit(solution)/shard_map/ppermute | solution.py:14
  59.9 6.6 copy.214
  66.5 4.9 reshape.50
  71.4 8.3 %pad_maximum_fusion = f32[2,2,512,1024]{3,2,1,0:T(8,128)} fusion(f32[2,2,256,1024]{3,2,1,0:T(8,128)} %reshape.50, f32[2,2,256,1024]{3,2,1,0:T(8,128)} %reshape.48), kind=kLoop, calls=%fused_computation.377 | loop fusion | flops 2097152 | bytes 16777216 | tf_op jit(solution)/shard_map/concatenate | solution.py:136
  79.7 4.3 broadcast_in_dim.2
  84.0 94.6 %while.12 = (s32[]{:T(128)}, f32[2,2,512,1024]{3,2,1,0:T(8,128)}, s32[]{:T(128)}, s32[2]{0:T(128)S(1)}, s32[]{:T(128)}, /*index=5*/s32[2]{0:T(128)S(1)}, f32[4,2...) while((s32[]{:T(128)}, f32[2,2,512,1024]{3,2,1,0:T(8,128)}, ...), condition=%wide.region_6.7_spmd.clone.clone, body=%wide.region_0.6_spmd.clone.clone.sunk | while | flops 6523715584 | bytes 125305184 | solution.py:161
  89.0 1.7 dynamic-slice_bitcast_fusion.5
  99.8 2.5 subtract_convert_fusion.7
  103.5 1.4 fusion.638
  111.3 1.5 subtract_convert_fusion.8
  115.3 1.5 fusion.646
  121.8 1.3 add_reduce_fusion.3
  129.2 1.7 fusion.653
  133.4 1.9 subtract_convert_fusion.9
  142.9 1.4 fusion.662
  144.3 2.4 add_convert_fusion.5
  155.5 1.6 fusion.670
  157.2 1.8 maximum_add_fusion.2
  159.1 12.2 %dynamic_update_slice.6 = f32[2,2,512,1024]{3,2,1,0:T(8,128)} dynamic-update-slice(f32[2,2,512,1024]{3,2,1,0:T(8,128)} %get-tuple-element.532, f32[2,2,256,256]{3,2,1,0:T(8,128)S(1)} %maximum_add_fusion.2, s32[]{:T(128)} %constant.10.clone.1..sunk, s32[]{:T(128)} %constant.10.clone.1..sunk, s32[]{:T(128)S(6)} %select_n.300, s32[]{:T(128)S(6)} %select_n.301) | dynamic-update-slice | bytes 2097156 | tf_op jit(solution)/shard_map/while/body/dynamic_update_slice | solution.py:158
  178.6 5.5 copy.211
  185.6 1.9 collective-permute-start.1
  188.4 44.6 %collective-permute-done.1 = f32[8192,128]{1,0:T(8,128)S(1)} collective-permute-done((f32[8192,128]{1,0:T(8,128)S(1)}, f32[8192,128]{1,0:T(8,128)S(1)}, u32[]{:S(2)}, u32[]{:S(2)}) %collective-permute-start.1) | collective-permute-done | bytes 4194336 | tf_op jit(solution)/shard_map/ppermute | solution.py:14
  233.0 2.4 bitcast_add_fusion
  235.4 416.7 %all-gather.3.cloned.1.call-done = f32[65536,128]{1,0:T(8,128)} async-done(((f32[8192,128]{1,0:T(8,128)}), f32[65536,128]{1,0:T(8,128)}) %all-gather.3.cloned.1.call-update) | async-done | bytes 33554448 | tf_op jit(solution)/shard_map/all_gather | solution.py:170
  652.2 14.0 %reduce_sum.56 = f32[8192,128]{1,0:T(8,128)} reduce(f32[8,8192,128]{2,1,0:T(8,128)} %bitcast.455, f32[]{:T(128)} %constant.11.clone.1), dimensions={0}, to_apply=%region_7.8 | reduce | flops 7340032 | bytes 37748740 | tf_op jit(solution)/shard_map/reduce_sum | solution.py:170
  666.2 2.7 broadcast_multiply_fusion
  669.6 2.8 sub.74
  (58 shorter events, 54.4 us)
Async XLA Ops:
  6.5 645.6 %all-gather.3.cloned.1.call-start = ((), (), s32[]{:S(2)}) async-start(), calls=%async_computation | async-start | bytes 37748736 | tf_op jit(solution)/shard_map/all_gather | solution.py:170
  6.5 53.4 %collective-permute-start = (f32[16,2,2,128,128]{4,3,2,1,0:T(8,128)}, f32[16,2,2,128,128]{4,3,2,1,0:T(8,128)}, u32[]{:S(2)}, u32[]{:S(2)}) collective-permute-start(f32[16,2,2,128,128]{4,3,2,1,0:T(8,128)} %param.9), channel_id=1, source_target_pairs={{8,0},{16,8},{24,16},{32,24},{40,32},{48,40},{56,48},{64,56},{72,6... | collective-permute-start | bytes 12582920 | tf_op jit(solution)/shard_map/ppermute | solution.py:14
  9.8 2.8 copy-start
  17.0 4.9 copy-start.2
  79.7 4.3 copy-start.3
  79.7 4.3 copy-start.4
  185.6 47.4 %collective-permute-start.1 = (f32[8192,128]{1,0:T(8,128)S(1)}, f32[8192,128]{1,0:T(8,128)S(1)}, u32[]{:S(2)}, u32[]{:S(2)}) collective-permute-start(f32[8192,128]{1,0:T(8,128)S(1)} %bitcast.465), channel_id=1, source_target_pairs={{0,8},{8,16},{16,24},{24,32},{32,40},{40,48},{48,56},{56,64},{64,7... | collective-permute-start | bytes 12582920 | tf_op jit(solution)/shard_map/ppermute | solution.py:14
  666.2 3.4 copy-start.1
Sparse Core Ops, SparseCore 0:
  235.6 416.5 all-gather.2
